TPU v7x, 256 devices: a whole 4x4x8 slice. The times are simulated.
256 devices in a mesh: probe: 4 (over y_lo, core), tile: 32 (over z, x), level: 2 (over y_hi).
Axes of the slice: x: 4, y: 4 (y_hi: 2, y_lo: 2; y = y_hi * 2 + y_lo), z: 8, core: 2. Of those that a mesh axis runs over, the one named last changes fastest.
Arguments:
- probe_bits: int32 [4, 64, 256, 256], P('probe', 'level', 'tile'), may hold values from 0 to 1
- kappa_sq: float32 [64, 256, 256], P('level', 'tile'), may hold values from 0.25 to 4
- observed: float32 [64, 256, 256], P('level', 'tile'), may hold values from -0.6 to 0.6
Outputs:
- gradient: float32 [64, 256, 256], P('level', 'tile', 'probe')
Inputs may be any that keep to these rules, and one draw needn't show every extreme that they name: `probe_bits`: a probe's sign is 2 times its bit minus 1.
All inputs are finite; a program needn't handle non-finite values.
Results may differ from a plain program's by a relative error of at most 0.0003.
Values sent between devices are 32-bit elements; how exact they have to be, the bound alone decides.
A program may use at most 64 MiB of HBM per device.

v0:
```python
import jax
import jax.numpy as jnp
from jax import lax
from jax.sharding import PartitionSpec as P

ITERS = 4
VERTICAL = 2.0


def with_halo(cells, sides, width):
    for axis, dim in sides:
        count = lax.axis_size(axis)
        ends = count - 1
        head = lax.slice_in_dim(cells, 0, width, axis=dim)
        tail = lax.slice_in_dim(cells, cells.shape[dim] - width, cells.shape[dim], axis=dim)
        cells = jnp.concatenate(
            [
                lax.ppermute(tail, axis, [(i, (i + 1) % count) for i in range(ends)]),
                cells,
                lax.ppermute(head, axis, [((i + 1) % count, i) for i in range(ends)]),
            ],
            axis=dim,
        )
    return cells


def shift_levels(values, stride, level_dim, fill_value):
    level_count = values.shape[level_dim]
    widths = [(0, 0)] * values.ndim
    if stride > 0:
        widths[level_dim] = (stride, 0)
        padded = jnp.pad(values, widths, constant_values=fill_value)
        return lax.slice_in_dim(padded, 0, level_count, axis=level_dim)
    widths[level_dim] = (0, -stride)
    padded = jnp.pad(values, widths, constant_values=fill_value)
    return lax.slice_in_dim(padded, -stride, level_count - stride, axis=level_dim)


def reduction_tables(kappa_sq):
    level_count = kappa_sq.shape[0]
    level_ids = lax.broadcasted_iota(jnp.int32, kappa_sq.shape, 0)
    diagonal = kappa_sq + (4.0 + 2.0 * VERTICAL)
    lower = jnp.where(level_ids > 0, -VERTICAL, 0.0).astype(jnp.float32)
    upper = jnp.where(level_ids < level_count - 1, -VERTICAL, 0.0).astype(jnp.float32)
    tables = []
    stride = 1
    while stride < level_count:
        lower_ratio = -lower / shift_levels(diagonal, stride, 0, 1.0)
        upper_ratio = -upper / shift_levels(diagonal, -stride, 0, 1.0)
        new_diagonal = (
            diagonal
            + lower_ratio * shift_levels(upper, stride, 0, 0.0)
            + upper_ratio * shift_levels(lower, -stride, 0, 0.0)
        )
        new_lower = lower_ratio * shift_levels(lower, stride, 0, 0.0)
        upper = upper_ratio * shift_levels(upper, -stride, 0, 0.0)
        lower = new_lower
        diagonal = new_diagonal
        tables.append((lower_ratio, upper_ratio, stride))
        stride = stride * 2
    return (tables, 1.0 / diagonal)


def vertical_solve(values, tables, inverse_diagonal):
    for lower_ratio, upper_ratio, stride in tables:
        values = (
            values
            + lower_ratio * shift_levels(values, stride, 1, 0.0)
            + upper_ratio * shift_levels(values, -stride, 1, 0.0)
        )
    return values * inverse_diagonal


def stencil(padded, values, kappa_sq):
    beside_x = padded[:, 1:-1, 2:, 1:-1] + padded[:, 1:-1, :-2, 1:-1]
    beside_y = padded[:, 1:-1, 1:-1, 2:] + padded[:, 1:-1, 1:-1, :-2]
    beside_z = padded[:, 2:, 1:-1, 1:-1] + padded[:, :-2, 1:-1, 1:-1]
    return (kappa_sq + (4.0 + 2.0 * VERTICAL)) * values - beside_x - beside_y - VERTICAL * beside_z


def slab_apply(values, kappa_sq):
    extended = with_halo(values, (("tile", 2), ("level", 1)), 1)
    padded = jnp.pad(extended, ((0, 0), (0, 0), (0, 0), (1, 1)))
    return stencil(padded, values, kappa_sq)


def local_dots(first, second):
    return jnp.sum(first * second, axis=(1, 2, 3))


def precond_total(residual, precond):
    return lax.psum(local_dots(residual, precond), ("tile", "level"))


def conjugate_solve(right_side, apply_q, apply_m):
    shaped = (right_side.shape[0], 1, 1, 1)
    solution = jnp.zeros_like(right_side)
    residual = right_side
    precond = apply_m(residual)
    rho_now = precond_total(residual, precond)
    direction = precond
    for iteration in range(ITERS):
        image_field = apply_q(direction)
        curv_total = lax.psum(local_dots(direction, image_field), ("tile", "level"))
        step_size = (rho_now / curv_total).reshape(shaped)
        solution = solution + step_size * direction
        if iteration + 1 < ITERS:
            residual = residual - step_size * image_field
            precond = apply_m(residual)
            rho_next = precond_total(residual, precond)
            direction = precond + (rho_next / rho_now).reshape(shaped) * direction
            rho_now = rho_next
    return solution


def body(probe_bits, kappa_sq, observed):
    sign_field = (2 * probe_bits - 1).astype(jnp.float32)
    stacked = jnp.concatenate([sign_field, observed[None]], axis=0)
    extended = with_halo(stacked, (("tile", 2), ("level", 1)), 1)
    padded = jnp.pad(extended, ((0, 0), (0, 0), (0, 0), (1, 1)))
    k_stacked = stencil(padded, stacked, kappa_sq)
    k_signs = k_stacked[:-1]
    data_term = 2.0 * observed * k_stacked[-1]
    kappa_cols = lax.all_to_all(kappa_sq[None], "level", split_axis=3, concat_axis=1, tiled=True)[0]
    tables, inverse_diagonal = reduction_tables(kappa_cols)

    def solve_columns(columns):
        solved = vertical_solve(
            vertical_solve(columns, tables, inverse_diagonal), tables, inverse_diagonal
        )
        return lax.all_to_all(solved, "level", split_axis=1, concat_axis=3, tiled=True)

    def apply_m(values):
        return solve_columns(
            lax.all_to_all(values, "level", split_axis=3, concat_axis=1, tiled=True)
        )

    def apply_q(values):
        return slab_apply(slab_apply(values, kappa_sq), kappa_sq)

    solution = conjugate_solve(sign_field, apply_q, apply_m)
    probe_partial = jnp.sum(
        solution * k_signs + slab_apply(solution, kappa_sq) * sign_field, axis=0
    )
    summed = lax.psum_scatter(probe_partial, "probe", scatter_dimension=2, tiled=True)
    y_width = summed.shape[2]
    offset = lax.axis_index("probe") * y_width
    kappa_part = lax.dynamic_slice_in_dim(kappa_sq, offset, y_width, 2)
    data_part = lax.dynamic_slice_in_dim(data_term, offset, y_width, 2)
    probe_count = probe_bits.shape[0] * lax.axis_size("probe")
    return kappa_part * (summed / probe_count - data_part)


def solution(mesh):
    in_specs = (
        P("probe", "level", "tile", None),
        P("level", "tile", None),
        P("level", "tile", None),
    )
    out_specs = P("level", "tile", "probe")
    return jax.shard_map(body, mesh=mesh, in_specs=in_specs, out_specs=out_specs, check_vma=False)
```

profile of v0, /device:TPU:1, one launch (start us, length us, event | category | flops | bytes accessed | tf_op | source)
XLA Modules:
  0.0 1670.7 jit_solution(17637381411247329690)
XLA Ops:
  9.1 5.0 all-to-all-start.1
  15.8 3.9 all-to-all-done.1
  19.7 3.4 all-to-all-start
  26.1 2.6 all-to-all-done
  33.5 8.0 all_to_all.165
  43.0 4.0 collective-permute-start.1
  51.2 4.7 collective-permute-done.3
  58.1 4.3 collective-permute-start.5
  66.3 4.7 collective-permute-done.7
  73.2 158.1 %all-reduce.140 = (f32[1]{0:T(128)}, f32[1]{0:T(128)}) all-reduce(f32[1]{0:T(128)} %bitcast.26, f32[1]{0:T(128)} %bitcast.30), channel_id=1, replica_groups=mesh['probe'=4,'tile'=32,'level'=2] {'tile','level'}, use_global_device_ids=true, to_apply=%region_1.2 | all-reduce | flops 2 | bytes 16 | tf_op jit(solution)/shard_map/psum | solution.py:92
  239.0 9.9 all_to_all.166
  249.0 3.1 reduce.10
  252.0 2.4 reshape.184
  259.4 8.0 all_to_all.167
  268.1 149.1 %psum.58 = f32[1]{0:T(128)} all-reduce(f32[1]{0:T(128)} %bitcast.39), channel_id=1, replica_groups=mesh['probe'=4,'tile'=32,'level'=2] {'tile','level'}, use_global_device_ids=true, to_apply=%region_5.6 | all-reduce | flops 1 | bytes 8 | tf_op jit(solution)/shard_map/psum | solution.py:92
  420.8 4.0 collective-permute-start.9
  425.9 5.0 collective-permute-start.10
  432.2 5.0 collective-permute-done.11
  440.1 4.0 collective-permute-start.13
  448.0 4.7 collective-permute-done.15
  454.8 149.1 %psum.59 = f32[1]{0:T(128)} all-reduce(f32[1]{0:T(128)} %bitcast.43), channel_id=1, replica_groups=mesh['probe'=4,'tile'=32,'level'=2] {'tile','level'}, use_global_device_ids=true, to_apply=%region_7.8 | all-reduce | flops 1 | bytes 8 | tf_op jit(solution)/shard_map/psum | solution.py:104
  611.7 10.3 all_to_all.168
  622.0 3.1 reduce.11
  625.1 2.4 reshape.186
  632.5 7.9 all_to_all.169
  641.7 149.8 %psum.60 = f32[1]{0:T(128)} all-reduce(f32[1]{0:T(128)} %bitcast.52), channel_id=1, replica_groups=mesh['probe'=4,'tile'=32,'level'=2] {'tile','level'}, use_global_device_ids=true, to_apply=%region_9.10 | all-reduce | flops 1 | bytes 8 | tf_op jit(solution)/shard_map/psum | solution.py:92
  795.2 4.0 collective-permute-start.17
  800.2 4.4 collective-permute-start.18
  805.9 4.7 collective-permute-done.19
  812.8 4.3 collective-permute-start.21
  821.1 5.0 collective-permute-done.23
  828.2 149.4 %psum.61 = f32[1]{0:T(128)} all-reduce(f32[1]{0:T(128)} %bitcast.56), channel_id=1, replica_groups=mesh['probe'=4,'tile'=32,'level'=2] {'tile','level'}, use_global_device_ids=true, to_apply=%region_11.12 | all-reduce | flops 1 | bytes 8 | tf_op jit(solution)/shard_map/psum | solution.py:104
  985.3 10.2 all_to_all.170
  995.5 3.1 reduce.12
  1006.0 8.1 all_to_all.171
  1014.8 150.4 %psum.62 = f32[1]{0:T(128)} all-reduce(f32[1]{0:T(128)} %bitcast.65), channel_id=1, replica_groups=mesh['probe'=4,'tile'=32,'level'=2] {'tile','level'}, use_global_device_ids=true, to_apply=%region_13.14 | all-reduce | flops 1 | bytes 8 | tf_op jit(solution)/shard_map/psum | solution.py:92
  1167.8 4.0 collective-permute-start.25
  1172.9 4.1 collective-permute-start.26
  1179.7 4.3 collective-permute-start.33
  1186.2 4.0 collective-permute-start.29
  1191.2 5.6 collective-permute-start.30
  1198.2 5.5 collective-permute-start.34
  1206.5 152.8 %psum.63 = f32[1]{0:T(128)} all-reduce(f32[1]{0:T(128)} %bitcast.69), channel_id=1, replica_groups=mesh['probe'=4,'tile'=32,'level'=2] {'tile','level'}, use_global_device_ids=true, to_apply=%region_15.16 | all-reduce | flops 1 | bytes 8 | tf_op jit(solution)/shard_map/psum | solution.py:104
  1362.0 4.0 collective-permute-start.37
  1371.2 3.9 collective-permute-done.39
  1376.1 4.4 copy.71
  1380.5 4.7 reshape.177
  1385.2 275.9 %reduce-scatter.4.cloned.1.call-done = f32[64,256]{1,0:T(8,128)} async-done(((f32[256,256]{1,0:T(8,128)}), f32[64,256]{1,0:T(8,128)}) %reduce-scatter.4.cloned.1.call-update) | async-done | bytes 65552
  (253 shorter events, 113.9 us)
Async XLA Ops:
  9.1 10.5 all-to-all-start.1
  19.7 9.0 all-to-all-start
  23.1 1637.9 %reduce-scatter.4.cloned.1.call-start = ((), (), s32[]{:S(2)}) async-start(), calls=%async_computation.10 | async-start | bytes 327680
  41.7 5.3 collective-permute-start
  43.0 5.0 collective-permute-start.1
  48.0 3.2 collective-permute-start.2
  49.9 6.0 collective-permute-start.3
  56.8 5.6 collective-permute-start.4
  58.1 5.3 collective-permute-start.5
  63.4 3.0 collective-permute-start.6
  65.0 6.0 collective-permute-start.7
  419.5 5.3 collective-permute-start.8
  420.8 5.0 collective-permute-start.9
  425.9 6.3 collective-permute-start.10
  430.9 6.3 collective-permute-start.11
  438.8 5.3 collective-permute-start.12
  440.1 5.0 collective-permute-start.13
  445.1 2.9 collective-permute-start.14
  446.7 6.0 collective-permute-start.15
  793.9 5.3 collective-permute-start.16
  795.2 5.0 collective-permute-start.17
  800.2 5.7 collective-permute-start.18
  804.6 6.0 collective-permute-start.19
  811.5 5.6 collective-permute-start.20
  812.8 5.3 collective-permute-start.21
  818.1 3.0 collective-permute-start.22
  819.7 6.3 collective-permute-start.23
  1005.9 172.4 %copy-start.10 = (f32[1,32,8,256]{3,2,1,0:T(8,128)S(1)}, f32[1,32,8,256]{3,2,1,0:T(8,128)}, u32[]{:S(2)}) copy-start(f32[1,32,8,256]{3,2,1,0:T(8,128)} %copy-done.9) | copy-start | bytes 786436
  1005.9 172.4 %copy-start.14 = (f32[32,8,256]{2,1,0:T(8,128)S(1)}, f32[32,8,256]{2,1,0:T(8,128)}, u32[]{:S(2)}) copy-start(f32[32,8,256]{2,1,0:T(8,128)} %param.5) | copy-start | bytes 786436
  1014.8 169.8 %copy-start.13 = (f32[1,64,8,128]{3,2,0,1:T(8,128)S(1)}, f32[1,64,8,128]{3,2,0,1:T(8,128)}, u32[]{:S(2)}) copy-start(f32[1,64,8,128]{3,2,0,1:T(8,128)} %copy-done.11) | copy-start | bytes 786436
  1014.8 169.8 %copy-start.23 = (f32[32,8,256]{2,1,0:T(8,128)S(1)}, f32[32,8,256]{2,1,0:T(8,128)}, u32[]{:S(2)}) copy-start(f32[32,8,256]{2,1,0:T(8,128)} %get-tuple-element.14) | copy-start | bytes 786436
  1166.5 5.3 collective-permute-start.24
  1167.8 5.0 collective-permute-start.25
  1172.9 11.1 collective-permute-start.26
  1177.0 7.0 collective-permute-start.27
  1178.4 19.8 %collective-permute-start.32 = (f32[2,32,1,256]{3,2,1,0:T(1,128)S(1)}, f32[2,32,1,256]{3,2,1,0:T(1,128)S(1)}, u32[]{:S(2)}, u32[]{:S(2)}) collective-permute-start(f32[2,32,1,256]{3,2,1,0:T(1,128)S(1)} %get-tuple-element.47), channel_id=1, source_target_pairs={{2,0},{4,2},{6,4},{8,6},{10,8},{12,10},{14,12},{16,14},{18,16},{20... | collective-permute-start | bytes 196616 | tf_op jit(solution)/shard_map/ppermute | solution.py:20
  1179.7 18.5 %collective-permute-start.33 = (f32[2,32,1,256]{3,2,1,0:T(1,128)S(1)}, f32[2,32,1,256]{3,2,1,0:T(1,128)S(1)}, u32[]{:S(2)}, u32[]{:S(2)}) collective-permute-start(f32[2,32,1,256]{3,2,1,0:T(1,128)S(1)} %get-tuple-element.46), channel_id=1, source_target_pairs={{0,2},{2,4},{4,6},{6,8},{8,10},{10,12},{12,14},{14,16},{16,18},{18... | collective-permute-start | bytes 196616 | tf_op jit(solution)/shard_map/ppermute | solution.py:18
  1184.9 5.3 collective-permute-start.28
  1186.2 5.0 collective-permute-start.29
  1191.2 169.4 %copy-start.6 = (f32[1,32,8,256]{3,2,1,0:T(8,128)S(1)}, f32[1,32,8,256]{3,2,1,0:T(8,128)}, u32[]{:S(2)}) copy-start(f32[1,32,8,256]{3,2,1,0:T(8,128)} %copy-done.5) | copy-start | bytes 786436
  1191.2 13.8 collective-permute-start.30
  1196.9 8.2 collective-permute-start.31
  1198.2 167.8 %collective-permute-start.34 = (f32[2,1,10,256]{3,2,1,0:T(8,128)S(1)}, f32[2,1,10,256]{3,2,1,0:T(8,128)S(1)}, u32[]{:S(2)}, u32[]{:S(2)}) collective-permute-start(f32[2,1,10,256]{3,2,1,0:T(8,128)S(1)} %get-tuple-element.39), channel_id=1, source_target_pairs={{0,1},{2,3},{4,5},{6,7},{8,9},{10,11},{12,13},{14,15},{16,17},{18,... | collective-permute-start | bytes 61448 | tf_op jit(solution)/shard_map/ppermute | solution.py:18
  1203.7 162.3 %collective-permute-start.35 = (f32[2,1,10,256]{3,2,1,0:T(8,128)S(1)}, f32[2,1,10,256]{3,2,1,0:T(8,128)S(1)}, u32[]{:S(2)}, u32[]{:S(2)}) collective-permute-start(f32[2,1,10,256]{3,2,1,0:T(8,128)S(1)} %get-tuple-element.38), channel_id=1, source_target_pairs={{1,0},{3,2},{5,4},{7,6},{9,8},{11,10},{13,12},{15,14},{17,16},{19,... | collective-permute-start | bytes 61448 | tf_op jit(solution)/shard_map/ppermute | solution.py:20
  1360.7 6.3 collective-permute-start.36
  1362.0 5.0 collective-permute-start.37
  1367.1 4.1 collective-permute-start.38
  1369.0 6.1 collective-permute-start.39
  (20 other events, 378.9 us)
Sparse Core Ops, SparseCore 0:
  1385.3 275.7 reduce-scatter.3
where the time goes:
time: 1670 us
  blocking collectives  1120 us (67%)
  waiting for transfers between devices  323 us (19%)
  starting transfers between devices  109 us (7%)
  local copies, waits for them, and re-layouts  52.3 us (3%)
  other arithmetic  41.6 us (2%)
  between operations  23.8 us (1%)
    psum x4, blocking collectives, precond_total(): return lax.psum(local_dots(residual, precond), ('tile', 'level'))  607 us
    psum x3, blocking collectives, conjugate_solve(): curv_total = lax.psum(local_dots(direction, image_field), ('tile', 'level'))  451 us
    unnamed x2, waiting for transfers between devices  276 us
    ppermute x20, starting transfers between devices, with_halo(): lax.ppermute(tail, axis, [(i, (i + 1) % count) for i in range(ends)])  74.2 us
  transfers between devices with their start and end apart: 43, of which 18 were waited for; matrix products, arithmetic and copies ran while one was open for 1% of the time, Pallas kernels for 0%

commit v1 on v0

--- a/solution.py
+++ b/solution.py
@@ -2,6 +2,7 @@
 import jax.numpy as jnp
 from jax import lax
 from jax.sharding import PartitionSpec as P
+from jax.lax import psum
 
 ITERS = 4
 VERTICAL = 2.0
@@ -101,7 +102,12 @@
     direction = precond
     for iteration in range(ITERS):
         image_field = apply_q(direction)
-        curv_total = lax.psum(local_dots(direction, image_field), ("tile", "level"))
+
+        def end_packet_in(here_x):
+            tile_out = psum(here_x, axis_name="tile")
+            return psum(tile_out, axis_name="level")
+
+        curv_total = end_packet_in(local_dots(direction, image_field))
         step_size = (rho_now / curv_total).reshape(shaped)
         solution = solution + step_size * direction
         if iteration + 1 < ITERS:

time: 1670 us -> 1460 us (0.87)
  blocking collectives: 1120 us -> 932 us
  waiting for transfers between devices: 323 us -> 286 us
    psum x3 -> x8, blocking collectives: 451 us -> 272 us  [the longest x4 247 us: end_packet_in(): tile_out = psum(here_x, axis_name='tile')]
    unnamed x2, waiting for transfers between devices: 276 us -> 240 us
where the time goes in v1:
time: 1460 us; the launch traced here: 1450 us
  blocking collectives  932 us (64%)
  waiting for transfers between devices  286 us (20%)
  starting transfers between devices  113 us (8%)
  local copies, waits for them, and re-layouts  52.3 us (4%)
  other arithmetic  43.2 us (3%)
  between operations  24.3 us (2%)
    psum x4, blocking collectives, precond_total(): return lax.psum(local_dots(residual, precond), ('tile', 'level'))  598 us
    psum x4, blocking collectives, end_packet_in(): tile_out = psum(here_x, axis_name='tile')  247 us
    unnamed x2, waiting for transfers between devices  240 us
    ppermute x20, starting transfers between devices, with_halo(): lax.ppermute(tail, axis, [(i, (i + 1) % count) for i in range(ends)])  78.6 us
    unnamed x72, local copies, waits for them, and re-layouts  33.4 us
    all_to_all x4, blocking collectives, solve_columns(): lax.all_to_all(solved, 'level', split_axis=1, concat_axis=3, tiled=True)  32.3 us
    ppermute x20, waiting for transfers between devices, with_halo(): lax.ppermute(head, axis, [((i + 1) % count, i) for i in range(ends)])  32.2 us
    all_to_all x3, blocking collectives, apply_m(): lax.all_to_all(values, 'level', split_axis=3, concat_axis=1, tiled=True)  29.7 us
  transfers between devices with their start and end apart: 43, of which 18 were waited for; matrix products, arithmetic and copies ran while one was open for 1% of the time, Pallas kernels for 0%

profile of v1, /device:TPU:1, one launch (start us, length us, event | category | flops | bytes accessed | tf_op | source)
XLA Modules:
  0.0 1451.1 jit_solution(6833126814067421161)
XLA Ops:
  9.2 5.0 all-to-all-start.1
  15.8 3.9 all-to-all-done.1
  19.7 3.4 all-to-all-start
  33.5 8.0 all_to_all.165
  42.9 4.0 collective-permute-start.1
  51.2 4.7 collective-permute-done.3
  58.0 4.3 collective-permute-start.5
  66.3 4.7 collective-permute-done.7
  73.2 65.8 %psum.85 = f32[1]{0:T(128)} all-reduce(f32[1]{0:T(128)} %bitcast.30), channel_id=1, replica_groups=mesh['probe'=4,'tile'=32,'level'=2] {'tile'}, use_global_device_ids=true, to_apply=%region_3.4 | all-reduce | flops 1 | bytes 8 | tf_op jit(solution)/shard_map/psum | solution.py:107
  138.9 5.9 psum.86
  144.8 149.8 %psum.84 = f32[1]{0:T(128)} all-reduce(f32[1]{0:T(128)} %bitcast.26), channel_id=1, replica_groups=mesh['probe'=4,'tile'=32,'level'=2] {'tile','level'}, use_global_device_ids=true, to_apply=%region_1.2 | all-reduce | flops 1 | bytes 8 | tf_op jit(solution)/shard_map/psum | solution.py:93
  302.3 10.2 all_to_all.166
  323.0 8.3 all_to_all.167
  332.0 149.6 %psum.87 = f32[1]{0:T(128)} all-reduce(f32[1]{0:T(128)} %bitcast.39), channel_id=1, replica_groups=mesh['probe'=4,'tile'=32,'level'=2] {'tile','level'}, use_global_device_ids=true, to_apply=%region_6.7 | all-reduce | flops 1 | bytes 8 | tf_op jit(solution)/shard_map/psum | solution.py:93
  485.2 4.0 collective-permute-start.9
  490.2 5.0 collective-permute-start.10
  496.5 4.7 collective-permute-done.11
  504.0 4.4 collective-permute-start.13
  512.4 5.0 collective-permute-done.15
  519.5 58.3 %psum.88 = f32[1]{0:T(128)} all-reduce(f32[1]{0:T(128)} %bitcast.43), channel_id=1, replica_groups=mesh['probe'=4,'tile'=32,'level'=2] {'tile'}, use_global_device_ids=true, to_apply=%region_8.9 | all-reduce | flops 1 | bytes 8 | tf_op jit(solution)/shard_map/psum | solution.py:107
  577.8 6.0 psum.89
  591.6 9.7 all_to_all.168
  611.7 7.9 all_to_all.169
  621.1 149.2 %psum.90 = f32[1]{0:T(128)} all-reduce(f32[1]{0:T(128)} %bitcast.52), channel_id=1, replica_groups=mesh['probe'=4,'tile'=32,'level'=2] {'tile','level'}, use_global_device_ids=true, to_apply=%region_11.12 | all-reduce | flops 1 | bytes 8 | tf_op jit(solution)/shard_map/psum | solution.py:93
  774.0 4.0 collective-permute-start.17
  779.1 5.1 collective-permute-start.18
  785.4 5.0 collective-permute-done.19
  792.6 4.0 collective-permute-start.21
  800.6 4.7 collective-permute-done.23
  807.4 59.1 %psum.91 = f32[1]{0:T(128)} all-reduce(f32[1]{0:T(128)} %bitcast.56), channel_id=1, replica_groups=mesh['probe'=4,'tile'=32,'level'=2] {'tile'}, use_global_device_ids=true, to_apply=%region_13.14 | all-reduce | flops 1 | bytes 8 | tf_op jit(solution)/shard_map/psum | solution.py:107
  866.4 6.1 psum.92
  880.4 9.8 all_to_all.170
  900.6 8.0 all_to_all.171
  909.3 149.2 %psum.93 = f32[1]{0:T(128)} all-reduce(f32[1]{0:T(128)} %bitcast.65), channel_id=1, replica_groups=mesh['probe'=4,'tile'=32,'level'=2] {'tile','level'}, use_global_device_ids=true, to_apply=%region_16.17 | all-reduce | flops 1 | bytes 8 | tf_op jit(solution)/shard_map/psum | solution.py:93
  1061.3 4.0 collective-permute-start.25
  1066.3 5.2 collective-permute-start.26
  1074.2 4.3 collective-permute-start.33
  1080.7 4.0 collective-permute-start.29
  1085.8 5.6 collective-permute-start.30
  1092.7 5.5 collective-permute-start.34
  1099.7 64.2 %psum.94 = f32[1]{0:T(128)} all-reduce(f32[1]{0:T(128)} %bitcast.69), channel_id=1, replica_groups=mesh['probe'=4,'tile'=32,'level'=2] {'tile'}, use_global_device_ids=true, to_apply=%region_18.19 | all-reduce | flops 1 | bytes 8 | tf_op jit(solution)/shard_map/psum | solution.py:107
  1165.2 6.8 psum.95
  1174.8 4.0 collective-permute-start.37
  1179.9 4.6 collective-permute-start.38
  1187.5 3.5 collective-permute-done.39
  1191.9 4.3 copy.71
  1196.3 4.7 reshape.177
  1201.0 240.2 %reduce-scatter.4.cloned.1.call-done = f32[64,256]{1,0:T(8,128)} async-done(((f32[256,256]{1,0:T(8,128)}), f32[64,256]{1,0:T(8,128)}) %reduce-scatter.4.cloned.1.call-update) | async-done | bytes 65552
  (264 shorter events, 129.6 us)
Async XLA Ops:
  9.2 10.5 all-to-all-start.1
  19.7 9.0 all-to-all-start
  23.1 1418.1 %reduce-scatter.4.cloned.1.call-start = ((), (), s32[]{:S(2)}) async-start(), calls=%async_computation.10 | async-start | bytes 327680
  41.6 5.3 collective-permute-start
  42.9 5.0 collective-permute-start.1
  47.9 3.2 collective-permute-start.2
  49.8 6.0 collective-permute-start.3
  56.7 5.6 collective-permute-start.4
  58.0 5.3 collective-permute-start.5
  63.3 3.0 collective-permute-start.6
  65.0 6.0 collective-permute-start.7
  483.9 5.3 collective-permute-start.8
  485.2 5.0 collective-permute-start.9
  490.2 6.3 collective-permute-start.10
  495.2 6.0 collective-permute-start.11
  502.7 5.7 collective-permute-start.12
  504.0 5.4 collective-permute-start.13
  509.4 3.0 collective-permute-start.14
  511.1 6.3 collective-permute-start.15
  772.7 5.3 collective-permute-start.16
  774.0 5.0 collective-permute-start.17
  779.1 6.4 collective-permute-start.18
  784.1 6.3 collective-permute-start.19
  791.3 5.3 collective-permute-start.20
  792.6 5.0 collective-permute-start.21
  797.6 3.0 collective-permute-start.22
  799.2 6.0 collective-permute-start.23
  900.4 159.5 %copy-start.8 = (f32[1,32,8,256]{3,2,1,0:T(8,128)S(1)}, f32[1,32,8,256]{3,2,1,0:T(8,128)}, u32[]{:S(2)}) copy-start(f32[1,32,8,256]{3,2,1,0:T(8,128)} %copy-done.7) | copy-start | bytes 786436
  900.5 172.3 %copy-start.10 = (f32[1,32,8,256]{3,2,1,0:T(8,128)S(1)}, f32[1,32,8,256]{3,2,1,0:T(8,128)}, u32[]{:S(2)}) copy-start(f32[1,32,8,256]{3,2,1,0:T(8,128)} %copy-done.9) | copy-start | bytes 786436
  900.5 172.3 %copy-start.14 = (f32[32,8,256]{2,1,0:T(8,128)S(1)}, f32[32,8,256]{2,1,0:T(8,128)}, u32[]{:S(2)}) copy-start(f32[32,8,256]{2,1,0:T(8,128)} %param.5) | copy-start | bytes 786436
  909.3 169.8 %copy-start.13 = (f32[1,64,8,128]{3,2,0,1:T(8,128)S(1)}, f32[1,64,8,128]{3,2,0,1:T(8,128)}, u32[]{:S(2)}) copy-start(f32[1,64,8,128]{3,2,0,1:T(8,128)} %copy-done.11) | copy-start | bytes 786436
  909.3 169.8 %copy-start.23 = (f32[32,8,256]{2,1,0:T(8,128)S(1)}, f32[32,8,256]{2,1,0:T(8,128)}, u32[]{:S(2)}) copy-start(f32[32,8,256]{2,1,0:T(8,128)} %get-tuple-element.12) | copy-start | bytes 786436
  1060.0 5.3 collective-permute-start.24
  1061.3 5.0 collective-permute-start.25
  1066.3 12.2 collective-permute-start.26
  1071.5 7.0 collective-permute-start.27
  1072.9 19.8 %collective-permute-start.32 = (f32[2,32,1,256]{3,2,1,0:T(1,128)S(1)}, f32[2,32,1,256]{3,2,1,0:T(1,128)S(1)}, u32[]{:S(2)}, u32[]{:S(2)}) collective-permute-start(f32[2,32,1,256]{3,2,1,0:T(1,128)S(1)} %get-tuple-element.45), channel_id=1, source_target_pairs={{2,0},{4,2},{6,4},{8,6},{10,8},{12,10},{14,12},{16,14},{18,16},{20... | collective-permute-start | bytes 196616 | tf_op jit(solution)/shard_map/ppermute | solution.py:21
  1074.2 18.5 %collective-permute-start.33 = (f32[2,32,1,256]{3,2,1,0:T(1,128)S(1)}, f32[2,32,1,256]{3,2,1,0:T(1,128)S(1)}, u32[]{:S(2)}, u32[]{:S(2)}) collective-permute-start(f32[2,32,1,256]{3,2,1,0:T(1,128)S(1)} %get-tuple-element.44), channel_id=1, source_target_pairs={{0,2},{2,4},{4,6},{6,8},{8,10},{10,12},{12,14},{14,16},{16,18},{18... | collective-permute-start | bytes 196616 | tf_op jit(solution)/shard_map/ppermute | solution.py:19
  1079.4 6.0 collective-permute-start.28
  1080.7 5.0 collective-permute-start.29
  1085.8 12.5 collective-permute-start.30
  1091.4 6.9 collective-permute-start.31
  1092.7 86.1 %collective-permute-start.34 = (f32[2,1,10,256]{3,2,1,0:T(8,128)S(1)}, f32[2,1,10,256]{3,2,1,0:T(8,128)S(1)}, u32[]{:S(2)}, u32[]{:S(2)}) collective-permute-start(f32[2,1,10,256]{3,2,1,0:T(8,128)S(1)} %get-tuple-element.37), channel_id=1, source_target_pairs={{0,1},{2,3},{4,5},{6,7},{8,9},{10,11},{12,13},{14,15},{16,17},{18,... | collective-permute-start | bytes 61448 | tf_op jit(solution)/shard_map/ppermute | solution.py:19
  1163.9 15.0 %collective-permute-start.35 = (f32[2,1,10,256]{3,2,1,0:T(8,128)S(1)}, f32[2,1,10,256]{3,2,1,0:T(8,128)S(1)}, u32[]{:S(2)}, u32[]{:S(2)}) collective-permute-start(f32[2,1,10,256]{3,2,1,0:T(8,128)S(1)} %get-tuple-element.36), channel_id=1, source_target_pairs={{1,0},{3,2},{5,4},{7,6},{9,8},{11,10},{13,12},{15,14},{17,16},{19,... | collective-permute-start | bytes 61448 | tf_op jit(solution)/shard_map/ppermute | solution.py:21
  1173.4 6.5 collective-permute-start.36
  1174.8 5.1 collective-permute-start.37
  1179.9 7.6 collective-permute-start.38
  1184.6 6.4 collective-permute-start.39
  (23 other events, 332.9 us)
Sparse Core Ops, SparseCore 0:
  1201.1 240.1 reduce-scatter.3
